TPU v7x, 32 devices: a whole 2x2x4 slice. The times are simulated.
32 devices in a mesh: dp: 8 (over z, core), tensor: 4 (over y, x).
Axes of the slice: x: 2, y: 2, z: 4, core: 2. Of those that a mesh axis runs over, the one named last changes fastest.
Arguments:
- block_input: bfloat16 [8192, 2048], P('dp'), may hold values from -6 to 6
- block_owner: int32 [64], P('dp'), may hold values from 0 to 63, as said below
- token_mask: int32 [8192], P('dp'), may hold values from 0 to 1, as said below
- attention_gain: float32 [2048], replicated, may hold values from 0.5 to 1.5
- query_weight: bfloat16 [2048, 2048], P(None, 'tensor')
- key_weight: bfloat16 [2048, 2048], P(None, 'tensor')
- value_weight: bfloat16 [2048, 2048], P(None, 'tensor'), may hold values from -0.125 to 0.125
- output_weight: bfloat16 [2048, 2048], P('tensor'), may hold values from -0.5 to 0.5
- feedforward_gain: float32 [2048], replicated, may hold values from 0.5 to 1.5
- gate_weight: bfloat16 [2048, 8192], P(None, 'tensor'), may hold values from -0.125 to 0.125
- up_weight: bfloat16 [2048, 8192], P(None, 'tensor'), may hold values from -0.125 to 0.125
- down_weight: bfloat16 [8192, 2048], P('tensor'), may hold values from -0.0625 to 0.0625
- cotangent: bfloat16 [8192, 2048], P('dp'), may hold values from -6 to 6
Outputs:
- block_output: bfloat16 [8192, 2048], P('dp')
- input_gradient: float32 [8192, 2048], P('dp')
- attention_gain_gradient: float32 [2048], P('dp')
- query_gradient: float32 [2048, 2048], P('dp', 'tensor')
- key_gradient: float32 [2048, 2048], P('dp', 'tensor')
- value_gradient: float32 [2048, 2048], P('dp', 'tensor')
- output_gradient: float32 [2048, 2048], P('tensor', 'dp')
- feedforward_gain_gradient: float32 [2048], P('dp')
- gate_gradient: float32 [2048, 8192], P('dp', 'tensor')
- up_gradient: float32 [2048, 8192], P('dp', 'tensor')
- down_gradient: float32 [8192, 2048], P('tensor', 'dp')
Inputs may be any that keep to these rules, and one draw needn't show every extreme that they name: `block_owner`: each sequence takes one to 4 consecutive blocks of a single index of dp; a block's entry is the index of its sequence's first block in the whole array. The first 4 blocks of every index of dp form one sequence. `token_mask`: in each sequence the real tokens come first and there is at least one unless the sequence is a single block of padding; the first sequence of every index of dp is all real (512 tokens). Blocks after the last real token of an index of dp are padding, each its own sequence.
All inputs are finite; a program needn't handle non-finite values.
Results may differ from a plain program's by a relative error of at most 0.014.
Values sent between devices are 32-bit elements; how exact they have to be, the bound alone decides.
No kernel may reach another device: no remote copies, remote signals or barrier semaphores. Data moves between devices by JAX's collectives and lax.ppermute only.
A program may use at most 384 MiB of HBM per device.

v0:
```python
import jax
import jax.numpy as jnp
from jax import lax
from jax.sharding import PartitionSpec as P

HD = 64
BLK = 128
GROUP = 512
WINDOW = 896
NORM_EPS = 1e-05
ROPE_BASE = 130000.0
MASKED = -1e30


def rms_forward(values, norm_gain):
    inverse = lax.rsqrt(jnp.mean(values * values, axis=-1, keepdims=True) + NORM_EPS)
    return (values * inverse * norm_gain, inverse)


def rms_backward(values, inverse, norm_gain, upstream):
    unit_rows = values * inverse
    gain_part = jnp.sum(upstream * unit_rows, axis=0)
    scaled = upstream * norm_gain
    back = inverse * (scaled - unit_rows * jnp.mean(scaled * unit_rows, axis=-1, keepdims=True))
    return (back, gain_part)


def rope_tables(positions, width):
    half_width = width // 2
    frequency = ROPE_BASE ** (-(jnp.arange(half_width, dtype=jnp.float32) * 2.0 / width))
    angles = positions.astype(jnp.float32)[:, None] * frequency[None, :]
    return (jnp.cos(angles)[:, None, :], jnp.sin(angles)[:, None, :])


def rotate(values, cosine, sine):
    half_width = values.shape[-1] // 2
    first_half = values[..., :half_width]
    second_half = values[..., half_width:]
    return jnp.concatenate(
        [first_half * cosine - second_half * sine, second_half * cosine + first_half * sine],
        axis=-1,
    )


def allowed_keys(query_owner, query_pos, key_owner, key_pos, key_valid):
    same = query_owner[:, None] == key_owner[None, :]
    causal = key_pos[None, :] <= query_pos[:, None]
    usable = (key_valid[None, :] > 0) | (key_pos[None, :] == 0)
    return same & causal & usable


def masked_scores(query_block, key_block, allowed, scale):
    scores = (
        jnp.einsum("qhd,khd->hqk", query_block, key_block, preferred_element_type=jnp.float32)
        * scale
    )
    return jnp.where(allowed[None], scores, MASKED)


def on_device(
    block_input,
    block_owner,
    token_mask,
    attention_gain,
    query_weight,
    key_weight,
    value_weight,
    output_weight,
    feedforward_gain,
    gate_weight,
    up_weight,
    down_weight,
    cotangent,
):
    row_count = block_input.shape[0]
    head_count = query_weight.shape[1] // HD
    scale = HD ** (-0.5)
    front = WINDOW - GROUP
    group_count = row_count // GROUP
    first_block = lax.axis_index("dp") * (row_count // BLK)
    owners = jnp.repeat(block_owner, BLK, total_repeat_length=row_count)
    row_index = jnp.arange(row_count, dtype=jnp.int32)
    positions = (row_index // BLK + first_block - owners) * BLK + row_index % BLK
    cosine, sine = rope_tables(positions, HD)
    key_owner = jnp.concatenate([jnp.full((front,), -1, jnp.int32), owners])
    key_pos = jnp.concatenate([jnp.zeros((front,), jnp.int32), positions])
    key_valid = jnp.concatenate([jnp.zeros((front,), jnp.int32), token_mask])
    group_masks = []
    for group in range(group_count):
        start = group * GROUP
        group_masks.append(
            allowed_keys(
                owners[start : start + GROUP],
                positions[start : start + GROUP],
                key_owner[start : start + WINDOW],
                key_pos[start : start + WINDOW],
                key_valid[start : start + WINDOW],
            )
        )
    inputs_f = block_input.astype(jnp.float32)
    normed_one, inverse_one = rms_forward(inputs_f, attention_gain)
    act_one = normed_one.astype(jnp.bfloat16)

    def project(weight):
        return jnp.dot(act_one, weight, preferred_element_type=jnp.float32).reshape(
            row_count, head_count, HD
        )

    queries = rotate(project(query_weight), cosine, sine).astype(jnp.bfloat16)
    keys_rot = rotate(project(key_weight), cosine, sine).astype(jnp.bfloat16)
    values_b = project(value_weight).astype(jnp.bfloat16)
    pad_block = jnp.zeros((front, head_count, HD), jnp.bfloat16)
    key_pad = jnp.concatenate([pad_block, keys_rot], axis=0)
    value_pad = jnp.concatenate([pad_block, values_b], axis=0)
    attn_list = []
    logsum_list = []
    for group in range(group_count):
        start = group * GROUP
        scores = masked_scores(
            queries[start : start + GROUP],
            key_pad[start : start + WINDOW],
            group_masks[group],
            scale,
        )
        peak = jnp.max(scores, axis=-1, keepdims=True)
        logsum = peak + jnp.log(jnp.sum(jnp.exp(scores - peak), axis=-1, keepdims=True))
        probs = jnp.exp(scores - logsum).astype(jnp.bfloat16)
        result = jnp.einsum(
            "hqk,khd->qhd",
            probs,
            value_pad[start : start + WINDOW],
            preferred_element_type=jnp.float32,
        )
        attn_list.append(result.astype(jnp.bfloat16))
        logsum_list.append(logsum)
    attn_heads = jnp.concatenate(attn_list, axis=0)
    attn_flat = attn_heads.reshape(row_count, head_count * HD)
    attn_part = jnp.dot(attn_flat, output_weight, preferred_element_type=jnp.float32)
    attn_total = lax.psum(attn_part, "tensor")
    hidden_sum = inputs_f + attn_total
    normed_two, inverse_two = rms_forward(hidden_sum, feedforward_gain)
    act_two = normed_two.astype(jnp.bfloat16)
    gate_pre = jnp.dot(act_two, gate_weight, preferred_element_type=jnp.float32)
    up_pre = jnp.dot(act_two, up_weight, preferred_element_type=jnp.float32)
    sigmoid_gate = jax.nn.sigmoid(gate_pre)
    inner = (gate_pre * sigmoid_gate * up_pre).astype(jnp.bfloat16)
    mlp_part = jnp.dot(inner, down_weight, preferred_element_type=jnp.float32)
    mlp_total = lax.psum(mlp_part, "tensor")
    block_output = (hidden_sum + mlp_total).astype(jnp.bfloat16)
    grad_rows = jnp.where(token_mask[:, None] > 0, cotangent, jnp.zeros_like(cotangent))
    down_grad = jnp.dot(inner.T, grad_rows, preferred_element_type=jnp.float32)
    inner_grad = jnp.dot(grad_rows, down_weight.T, preferred_element_type=jnp.float32)
    gate_back = (
        inner_grad * up_pre * sigmoid_gate * (1.0 + gate_pre * (1.0 - sigmoid_gate))
    ).astype(jnp.bfloat16)
    up_back = (inner_grad * gate_pre * sigmoid_gate).astype(jnp.bfloat16)
    gate_grad = jnp.dot(act_two.T, gate_back, preferred_element_type=jnp.float32)
    up_grad = jnp.dot(act_two.T, up_back, preferred_element_type=jnp.float32)
    act_two_part = jnp.dot(gate_back, gate_weight.T, preferred_element_type=jnp.float32) + jnp.dot(
        up_back, up_weight.T, preferred_element_type=jnp.float32
    )
    act_two_grad = lax.psum(act_two_part, "tensor")
    hidden_norm_back, second_gain_grad = rms_backward(
        hidden_sum, inverse_two, feedforward_gain, act_two_grad
    )
    hidden_grad = grad_rows.astype(jnp.float32) + hidden_norm_back
    mlp_summed = (
        lax.psum_scatter(gate_grad, "dp", scatter_dimension=0, tiled=True),
        lax.psum_scatter(up_grad, "dp", scatter_dimension=0, tiled=True),
        lax.psum_scatter(down_grad, "dp", scatter_dimension=1, tiled=True),
        lax.psum_scatter(second_gain_grad, "dp", scatter_dimension=0, tiled=True),
    )
    hidden_back = hidden_grad.astype(jnp.bfloat16)
    out_grad = jnp.dot(attn_flat.T, hidden_back, preferred_element_type=jnp.float32)
    attention_grad = (
        jnp.dot(hidden_back, output_weight.T, preferred_element_type=jnp.float32)
        .astype(jnp.bfloat16)
        .reshape(row_count, head_count, HD)
    )
    key_acc = jnp.zeros((front + row_count, head_count, HD), jnp.float32)
    value_acc = jnp.zeros((front + row_count, head_count, HD), jnp.float32)
    query_parts = []
    for group in range(group_count):
        start = group * GROUP
        query_block = queries[start : start + GROUP]
        key_block = key_pad[start : start + WINDOW]
        value_block = value_pad[start : start + WINDOW]
        grad_block = attention_grad[start : start + GROUP]
        scores = masked_scores(query_block, key_block, group_masks[group], scale)
        probs_f = jnp.exp(scores - logsum_list[group])
        probs_b = probs_f.astype(jnp.bfloat16)
        value_acc = value_acc.at[start : start + WINDOW].add(
            jnp.einsum("hqk,qhd->khd", probs_b, grad_block, preferred_element_type=jnp.float32)
        )
        prob_grad = jnp.einsum(
            "qhd,khd->hqk", grad_block, value_block, preferred_element_type=jnp.float32
        )
        delta = jnp.sum(
            grad_block.astype(jnp.float32) * attn_heads[start : start + GROUP].astype(jnp.float32),
            axis=-1,
        ).T[:, :, None]
        score_grad = (probs_f * (prob_grad - delta) * scale).astype(jnp.bfloat16)
        query_parts.append(
            jnp.einsum("hqk,khd->qhd", score_grad, key_block, preferred_element_type=jnp.float32)
        )
        key_acc = key_acc.at[start : start + WINDOW].add(
            jnp.einsum("hqk,qhd->khd", score_grad, query_block, preferred_element_type=jnp.float32)
        )
    query_back = (
        rotate(jnp.concatenate(query_parts, axis=0), cosine, -sine)
        .astype(jnp.bfloat16)
        .reshape(row_count, head_count * HD)
    )
    key_back = (
        rotate(key_acc[front:], cosine, -sine)
        .astype(jnp.bfloat16)
        .reshape(row_count, head_count * HD)
    )
    value_back = value_acc[front:].astype(jnp.bfloat16).reshape(row_count, head_count * HD)
    query_grad = jnp.dot(act_one.T, query_back, preferred_element_type=jnp.float32)
    key_grad = jnp.dot(act_one.T, key_back, preferred_element_type=jnp.float32)
    value_grad = jnp.dot(act_one.T, value_back, preferred_element_type=jnp.float32)
    act_one_part = (
        jnp.dot(query_back, query_weight.T, preferred_element_type=jnp.float32)
        + jnp.dot(key_back, key_weight.T, preferred_element_type=jnp.float32)
        + jnp.dot(value_back, value_weight.T, preferred_element_type=jnp.float32)
    )
    act_one_grad = lax.psum(act_one_part, "tensor")
    input_norm_back, first_gain_grad = rms_backward(
        inputs_f, inverse_one, attention_gain, act_one_grad
    )
    input_gradient = hidden_grad + input_norm_back
    first_summed = (
        lax.psum_scatter(first_gain_grad, "dp", scatter_dimension=0, tiled=True),
        lax.psum_scatter(query_grad, "dp", scatter_dimension=0, tiled=True),
        lax.psum_scatter(key_grad, "dp", scatter_dimension=0, tiled=True),
        lax.psum_scatter(value_grad, "dp", scatter_dimension=0, tiled=True),
        lax.psum_scatter(out_grad, "dp", scatter_dimension=1, tiled=True),
    )
    gate_sum, up_sum, down_sum, second_gain_sum = mlp_summed
    first_gain_sum, query_sum, key_sum, value_sum, out_sum = first_summed
    return (
        block_output,
        input_gradient,
        first_gain_sum,
        query_sum,
        key_sum,
        value_sum,
        out_sum,
        second_gain_sum,
        gate_sum,
        up_sum,
        down_sum,
    )


def solution(mesh):
    return jax.shard_map(
        on_device,
        mesh=mesh,
        in_specs=(
            P("dp", None),
            P("dp"),
            P("dp"),
            P(),
            P(None, "tensor"),
            P(None, "tensor"),
            P(None, "tensor"),
            P("tensor", None),
            P(),
            P(None, "tensor"),
            P(None, "tensor"),
            P("tensor", None),
            P("dp", None),
        ),
        out_specs=(
            P("dp", None),
            P("dp", None),
            P("dp"),
            P("dp", "tensor"),
            P("dp", "tensor"),
            P("dp", "tensor"),
            P("tensor", "dp"),
            P("dp"),
            P("dp", "tensor"),
            P("dp", "tensor"),
            P("tensor", "dp"),
        ),
        check_vma=False,
    )
```

profile of v0, /device:TPU:0, one launch (start us, length us, event | category | flops | bytes accessed | tf_op | source)
XLA Modules:
  0.0 1614.1 jit_solution(13321575594222905438)
XLA Ops:
  8.9 4.5 compare_select_fusion.1
  14.1 3.1 fusion.14
  17.2 5.5 fusion.72
  22.8 2.6 fusion.70
  28.0 2.8 fusion.6
  30.8 4.0 exponential_reduce_fusion.1
  34.8 2.6 convolution_convert_fusion
  38.0 6.8 fusion.7
  44.8 7.3 exponential_reduce_fusion
  52.3 4.1 fusion.24
  56.4 7.5 fusion.25
  65.7 5.8 fusion.81
  71.6 174.8 %all-reduce.15.cloned.1.call-done = f32[1024,2048]{1,0:T(8,128)} async-done(((f32[1024,2048]{1,0:T(8,128)}), f32[1024,2048]{1,0:T(8,128)}) %all-reduce.15.cloned.1.call-update) | async-done | bytes 8388624 | tf_op jit(solution)/shard_map/psum | solution.py:139
  246.5 5.7 multiply_reduce_fusion.2
  253.0 16.5 %fusion.82 = f32[1024,2048]{1,0:T(8,128)} fusion(bf16[1024,2048]{1,0:T(8,128)(2,1)S(1)} %multiply_convert_fusion.5, bf16[2048,2048]{1,0:T(8,128)(2,1)} %param.32), kind=kOutput, calls=%fused_computation.154 | convolution fusion | flops 8589934592 | bytes 20971520 | tf_op jit(solution)/shard_map/dot_general | solution.py:143
  269.5 13.3 fusion.83
  282.9 21.9 %multiply_convert_fusion.2 = (bf16[1024,2048]{1,0:T(8,128)(2,1)}, bf16[1024,2048]{1,0:T(8,128)(2,1)}, bf16[1024,2048]{1,0:T(8,128)(2,1)}) fusion(f32[1024,2048]{1,0:T(8,128)} %fusion.82, f32[1024,2048]{1,0:T(8,128)} %fusion.83, bf16[2048,2048]{1,0:T(8,128)(2,1)} %param.34, bf16[1024,2048]{1,0:T(8,128)(2,1)} %param.35, ...), kind=kOutput, calls=%fused_computation.30 | convolution fusion | flops 8625586176 | bytes 41944064 | tf_op jit(solution)/shard_map/dot_general | solution.py:152
  304.8 13.1 fusion.85
  317.9 13.6 convolution_add_fusion
  331.6 14.7 fusion.84
  346.3 158.2 %all-reduce.17.cloned.1.call-done = f32[1024,2048]{1,0:T(8,128)} async-done(((f32[1024,2048]{1,0:T(8,128)}), f32[1024,2048]{1,0:T(8,128)}) %all-reduce.17.cloned.1.call-update) | async-done | bytes 8388624 | tf_op jit(solution)/shard_map/psum | solution.py:162
  504.4 7.6 multiply_reduce_fusion
  512.1 9.5 multiply_add_fusion
  521.7 6.6 fusion.21
  528.8 4.0 convolution_bitcast_fusion
  532.9 7.6 multiply_convert_fusion.1
  540.5 5.6 convolution_bitcast_fusion.3
  547.8 7.4 fusion.19
  555.4 9.1 multiply_convert_fusion
  576.3 5.8 add_add_fusion
  582.9 7.2 fusion.64
  590.1 7.8 fusion.15
  598.0 7.0 fusion.66
  605.1 7.3 fusion.68
  612.6 15.6 fusion.88
  628.3 15.5 fusion.89
  644.2 15.6 fusion.62
  661.7 228.7 %all-reduce.19.cloned.1.call-done = (f32[1024,2048]{1,0:T(8,128)}, f32[1024,2048]{1,0:T(8,128)}) async-done(((f32[1024,2048]{1,0:T(8,128)}, f32[1024,2048]{1,0:T(8,128)}), (f32[1024,2048]{1,0:T(8,128)}, f32[1024,2048]{1,0:T(8,128)})) %all-reduce.19.cloned.1.call-update) | async-done | bytes 16777232 | tf_op jit(solution)/shard_map/psum | solution.py:148
  890.4 5.9 fusion.13
  896.2 29.6 %all-reduce.9 = (f32[2048]{0:T(1024)S(1)}, f32[2048]{0:T(1024)S(1)}) all-reduce(f32[2048]{0:T(1024)S(1)} %get-tuple-element.73, f32[2048]{0:T(1024)S(1)} %copy-done.47), channel_id=2, replica_groups=mesh['dp'=8,'tensor'=4] {'dp'}, use_global_device_ids=true, to_apply=%region_15.16.clone | all-reduce | flops 4096 | bytes 32768
  927.1 9.6 add_convert_fusion
  936.7 9.8 fusion.12
  946.6 49.2 %reduce-scatter.14.cloned.1.call-done = f32[512,256]{1,0:T(8,128)} async-done(((f32[512,2048]{1,0:T(8,128)}), f32[512,256]{1,0:T(8,128)}) %reduce-scatter.14.cloned.1.call-update) | async-done | bytes 524304 | tf_op jit(solution)/shard_map/reduce_scatter | solution.py:238
  995.8 51.1 %reduce-scatter.10.cloned.1.call-done = f32[256,512]{1,0:T(8,128)} async-done(((f32[2048,512]{1,0:T(8,128)}), f32[256,512]{1,0:T(8,128)}) %reduce-scatter.10.cloned.1.call-update) | async-done | bytes 524304 | tf_op jit(solution)/shard_map/reduce_scatter | solution.py:236
  1046.9 51.3 %reduce-scatter.8.cloned.1.call-done = f32[256,512]{1,0:T(8,128)} async-done(((f32[2048,512]{1,0:T(8,128)}), f32[256,512]{1,0:T(8,128)}) %reduce-scatter.8.cloned.1.call-update) | async-done | bytes 524304 | tf_op jit(solution)/shard_map/reduce_scatter | solution.py:235
  1098.2 169.6 %reduce-scatter.16.cloned.1.call-done = f32[256,2048]{1,0:T(8,128)} async-done(((f32[2048,2048]{1,0:T(8,128)}), f32[256,2048]{1,0:T(8,128)}) %reduce-scatter.16.cloned.1.call-update) | async-done | bytes 2097168 | tf_op jit(solution)/shard_map/reduce_scatter | solution.py:168
  1267.8 169.6 %reduce-scatter.18.cloned.1.call-done = f32[256,2048]{1,0:T(8,128)} async-done(((f32[2048,2048]{1,0:T(8,128)}), f32[256,2048]{1,0:T(8,128)}) %reduce-scatter.18.cloned.1.call-update) | async-done | bytes 2097168 | tf_op jit(solution)/shard_map/reduce_scatter | solution.py:169
  1437.4 169.4 %reduce-scatter.20.cloned.1.call-done = f32[2048,256]{1,0:T(8,128)} async-done(((f32[2048,2048]{1,0:T(8,128)}), f32[2048,256]{1,0:T(8,128)}) %reduce-scatter.20.cloned.1.call-update) | async-done | bytes 2097168 | tf_op jit(solution)/shard_map/reduce_scatter | solution.py:170
  (188 shorter events, 26.0 us)
Async XLA Ops:
  7.2 58.5 %copy-start = (bf16[512,2048]{1,0:T(8,128)(2,1)S(1)}, bf16[512,2048]{1,0:T(8,128)(2,1)}, u32[]{:S(2)}) copy-start(bf16[512,2048]{1,0:T(8,128)(2,1)} %param.30) | copy-start | bytes 6291460
  7.2 239.3 %all-reduce.15.cloned.1.call-start = ((), (), s32[]{:S(2)}) async-start(), calls=%async_computation.7 | async-start | bytes 16777216 | tf_op jit(solution)/shard_map/psum | solution.py:139
  17.2 17.6 %copy-start.44 = (f32[1024]{0:T(1024)}, f32[1024]{0:T(1024)S(1)}, u32[]{:S(2)}) copy-start(f32[1024]{0:T(1024)S(1)} %add_rsqrt_fusion.1) | copy-start | bytes 12292
  27.3 10.7 copy-start.9
  27.4 10.6 copy-start.11
  27.4 10.6 copy-start.13
  27.4 10.6 copy-start.15
  28.0 24.2 %copy-start.19 = (pred[512,896]{1,0:T(8,128)(4,1)}, pred[512,896]{1,0:T(8,128)(4,1)S(1)}, u32[]{:S(2)}) copy-start(pred[512,896]{1,0:T(8,128)(4,1)S(1)} %and_and_fusion.1) | copy-start | bytes 1376260
  30.8 21.4 %copy-start.5 = (f32[8,512,896]{2,1,0:T(8,128)}, f32[8,512,896]{2,1,0:T(8,128)S(1)}, u32[]{:S(2)}) copy-start(f32[8,512,896]{2,1,0:T(8,128)S(1)} %get-tuple-element.127) | copy-start | bytes 44040196
  34.8 17.4 %copy-start.52 = (f32[8,512]{1,0:T(8,128)}, f32[8,512]{1,0:T(8,128)S(1)}, u32[]{:S(2)}) copy-start(f32[8,512]{1,0:T(8,128)S(1)} %log_add_fusion.1) | copy-start | bytes 49156
  37.5 14.8 copy-start.39
  38.0 18.4 %copy-start.27 = (pred[512,896]{1,0:T(8,128)(4,1)}, pred[512,896]{1,0:T(8,128)(4,1)S(1)}, u32[]{:S(2)}) copy-start(pred[512,896]{1,0:T(8,128)(4,1)S(1)} %and_and_fusion) | copy-start | bytes 1376260
  56.4 7.5 copy-start.23
  71.5 432.9 %all-reduce.17.cloned.1.call-start = ((), (), s32[]{:S(2)}) async-start(), calls=%async_computation.8 | async-start | bytes 16777216 | tf_op jit(solution)/shard_map/psum | solution.py:162
  71.6 180.6 %copy-start.43 = (f32[2048]{0:T(1024)S(1)}, f32[2048]{0:T(1024)}, u32[]{:S(2)}) copy-start(f32[2048]{0:T(1024)} %param.31) | copy-start | bytes 24580
  252.2 17.4 %copy-start.2 = (f32[1024,2048]{1,0:T(8,128)}, f32[1024,2048]{1,0:T(8,128)S(1)}, u32[]{:S(2)}) copy-start(f32[1024,2048]{1,0:T(8,128)S(1)} %get-tuple-element.82) | copy-start | bytes 25165828
  253.0 16.6 %copy-start.17 = (bf16[1024,2048]{1,0:T(8,128)(2,1)}, bf16[1024,2048]{1,0:T(8,128)(2,1)S(1)}, u32[]{:S(2)}) copy-start(bf16[1024,2048]{1,0:T(8,128)(2,1)S(1)} %multiply_convert_fusion.5) | copy-start | bytes 12582916
  304.8 13.2 copy-start.58
  331.5 558.8 %all-reduce.19.cloned.1.call-start = ((), (), s32[]{:S(2)}) async-start(), calls=%async_computation.16 | async-start | bytes 33554432 | tf_op jit(solution)/shard_map/psum | solution.py:148
  504.4 7.6 copy-start.18
  512.1 16.7 %slice-start = ((s8[14680064]{0:T(1024)(128)(4,1)}), s8[4194304]{0:T(1024)(128)(4,1)S(1)}, s32[]{:S(2)}) async-start(s8[14680064]{0:T(1024)(128)(4,1)} %bitcast.98), calls=%async_computation.17 | async-start | bytes 8388608
  512.1 16.7 %slice-start.1 = ((s8[14680064]{0:T(1024)(128)(4,1)}), s8[4194304]{0:T(1024)(128)(4,1)S(1)}, s32[]{:S(2)}) async-start(s8[14680064]{0:T(1024)(128)(4,1)} %bitcast.98), calls=%async_computation.18 | async-start | bytes 8388608
  512.1 16.7 %slice-start.2 = ((s8[14680064]{0:T(1024)(128)(4,1)}), s8[4194304]{0:T(1024)(128)(4,1)S(1)}, s32[]{:S(2)}) async-start(s8[14680064]{0:T(1024)(128)(4,1)} %bitcast.98), calls=%async_computation.19 | async-start | bytes 8388608
  521.6 6.7 copy-start.24
  521.6 6.7 copy-start.26
  521.6 7.1 slice-start.3
  521.6 7.1 copy-start.20
  521.6 7.1 copy-start.53
  528.4 19.3 %copy-start.42 = (bf16[512,512]{0,1:T(8,128)(2,1)}, bf16[512,512]{0,1:T(8,128)(2,1)S(1)}, u32[]{:S(2)}) copy-start(bf16[512,512]{0,1:T(8,128)(2,1)S(1)} %get-tuple-element.98) | copy-start | bytes 1572868
  532.9 7.6 copy-start.8
  540.5 5.6 copy-start.10
  540.5 5.6 copy-start.12
  547.7 7.6 copy-start.38
  555.4 9.2 copy-start.14
  555.4 9.2 copy-start.16
  582.2 7.9 copy-start.32
  582.2 364.4 %reduce-scatter.12.cloned.1.call-start = ((), (), s32[]{:S(2)}) async-start(), calls=%async_computation.11 | async-start | bytes 4718592 | tf_op jit(solution)/shard_map/reduce_scatter | solution.py:237
  590.1 7.9 copy-start.36
  590.1 405.7 %reduce-scatter.14.cloned.1.call-start = ((), (), s32[]{:S(2)}) async-start(), calls=%async_computation.12 | async-start | bytes 4718592 | tf_op jit(solution)/shard_map/reduce_scatter | solution.py:238
  597.9 7.2 copy-start.34
  597.9 449.0 %reduce-scatter.10.cloned.1.call-start = ((), (), s32[]{:S(2)}) async-start(), calls=%async_computation.10 | async-start | bytes 4718592 | tf_op jit(solution)/shard_map/reduce_scatter | solution.py:236
  605.0 493.2 %reduce-scatter.8.cloned.1.call-start = ((), (), s32[]{:S(2)}) async-start(), calls=%async_computation.9 | async-start | bytes 4718592 | tf_op jit(solution)/shard_map/reduce_scatter | solution.py:235
  612.4 655.4 %reduce-scatter.16.cloned.1.call-start = ((), (), s32[]{:S(2)}) async-start(), calls=%async_computation.13 | async-start | bytes 18874368 | tf_op jit(solution)/shard_map/reduce_scatter | solution.py:168
  628.3 809.1 %reduce-scatter.18.cloned.1.call-start = ((), (), s32[]{:S(2)}) async-start(), calls=%async_computation.14 | async-start | bytes 18874368 | tf_op jit(solution)/shard_map/reduce_scatter | solution.py:169
  643.9 963.0 %reduce-scatter.20.cloned.1.call-start = ((), (), s32[]{:S(2)}) async-start(), calls=%async_computation.15 | async-start | bytes 18874368 | tf_op jit(solution)/shard_map/reduce_scatter | solution.py:170
  659.8 236.4 %copy-start.47 = (f32[2048]{0:T(1024)S(1)}, f32[2048]{0:T(1024)}, u32[]{:S(2)}) copy-start(f32[2048]{0:T(1024)} %get-tuple-element.71) | copy-start | bytes 24580
  927.1 9.6 copy-start.4
  927.1 679.7 %copy-start.1 = (bf16[512,2048]{1,0:T(8,128)(2,1)S(1)}, bf16[512,2048]{1,0:T(8,128)(2,1)}, u32[]{:S(2)}) copy-start(bf16[512,2048]{1,0:T(8,128)(2,1)} %param.30) | copy-start | bytes 6291460
  (25 other events, 68.0 us)
Sparse Core Ops, SparseCore 0:
  71.7 174.7 all-reduce.14
  331.7 172.7 all-reduce.16
  582.3 308.0 all-reduce.18
  893.1 51.4 reduce-scatter.11
  947.3 48.4 reduce-scatter.13
  998.5 48.3 reduce-scatter.9
  1049.8 48.3 reduce-scatter.7
  1101.2 166.6 reduce-scatter.15
  1270.8 166.6 reduce-scatter.17
  1440.2 166.6 reduce-scatter.19
where the time goes:
time: 1620 us; the launch traced here: 1610 us
  waiting for transfers between devices  1220 us (75%)
  matrix products  263 us (16%)
  other arithmetic  72.8 us (4%)
  blocking collectives  29.6 us (2%)
  between operations  16.4 us (1%)
    psum x1, waiting for transfers between devices, on_device(): mlp_total = lax.psum(mlp_part, 'tensor')  229 us
    psum x1, waiting for transfers between devices, on_device(): attn_total = lax.psum(attn_part, 'tensor')  175 us
    reduce_scatter x1, waiting for transfers between devices, on_device(): lax.psum_scatter(up_grad, 'dp', scatter_dimension=0, tiled=True)  170 us
    reduce_scatter x1, waiting for transfers between devices, on_device(): lax.psum_scatter(gate_grad, 'dp', scatter_dimension=0, tiled=True)  170 us
    reduce_scatter x1, waiting for transfers between devices, on_device(): lax.psum_scatter(down_grad, 'dp', scatter_dimension=1, tiled=True)  169 us
    psum x1, waiting for transfers between devices, on_device(): act_two_grad = lax.psum(act_two_part, 'tensor')  158 us
    reduce_scatter x1, waiting for transfers between devices, on_device(): lax.psum_scatter(query_grad, 'dp', scatter_dimension=0, tiled=True)  51.3 us
    reduce_scatter x1, waiting for transfers between devices, on_device(): lax.psum_scatter(key_grad, 'dp', scatter_dimension=0, tiled=True)  51.1 us
  transfers between devices with their start and end apart: 10, of which 9 were waited for; matrix products, arithmetic and copies ran while one was open for 7% of the time, Pallas kernels for 0%

commit v1 on v0

--- a/solution.py
+++ b/solution.py
@@ -136,7 +136,8 @@
     attn_heads = jnp.concatenate(attn_list, axis=0)
     attn_flat = attn_heads.reshape(row_count, head_count * HD)
     attn_part = jnp.dot(attn_flat, output_weight, preferred_element_type=jnp.float32)
-    attn_total = lax.psum(attn_part, "tensor")
+    terms = lax.all_gather(attn_part, "tensor", axis=0, tiled=False)
+    attn_total = terms.sum(axis=0)
     hidden_sum = inputs_f + attn_total
     normed_two, inverse_two = rms_forward(hidden_sum, feedforward_gain)
     act_two = normed_two.astype(jnp.bfloat16)

time: 1620 us -> 1760 us (1.086)
  waiting for transfers between devices: 1220 us -> 1350 us
    all_gather x0 -> x1, waiting for transfers between devices: none -> 300 us  [on_device(): terms = lax.all_gather(attn_part, 'tensor', axis=0, tiled=False)]
    psum x1 -> x0, waiting for transfers between devices: 175 us -> none  [on_device(): attn_total = lax.psum(attn_part, 'tensor')]
where the time goes in v1:
time: 1760 us; the launch traced here: 1750 us
  waiting for transfers between devices  1350 us (77%)
  matrix products  263 us (15%)
  other arithmetic  89.2 us (5%)
  blocking collectives  29.6 us (2%)
    all_gather x1, waiting for transfers between devices, on_device(): terms = lax.all_gather(attn_part, 'tensor', axis=0, tiled=False)  300 us
    psum x1, waiting for transfers between devices, on_device(): mlp_total = lax.psum(mlp_part, 'tensor')  229 us
    reduce_scatter x1, waiting for transfers between devices, on_device(): lax.psum_scatter(up_grad, 'dp', scatter_dimension=0, tiled=True)  170 us
    reduce_scatter x1, waiting for transfers between devices, on_device(): lax.psum_scatter(gate_grad, 'dp', scatter_dimension=0, tiled=True)  170 us
    reduce_scatter x1, waiting for transfers between devices, on_device(): lax.psum_scatter(down_grad, 'dp', scatter_dimension=1, tiled=True)  169 us
    psum x1, waiting for transfers between devices, on_device(): act_two_grad = lax.psum(act_two_part, 'tensor')  157 us
    reduce_scatter x1, waiting for transfers between devices, on_device(): lax.psum_scatter(query_grad, 'dp', scatter_dimension=0, tiled=True)  51.3 us
    reduce_scatter x1, waiting for transfers between devices, on_device(): lax.psum_scatter(key_grad, 'dp', scatter_dimension=0, tiled=True)  51.1 us
  transfers between devices with their start and end apart: 10, of which 9 were waited for; matrix products, arithmetic and copies ran while one was open for 7% of the time, Pallas kernels for 0%

profile of v1, /device:TPU:0, one launch (start us, length us, event | category | flops | bytes accessed | tf_op | source)
XLA Modules:
  0.0 1754.2 jit_solution(14434763133465057332)
XLA Ops:
  8.9 4.5 compare_select_fusion.1
  14.1 3.1 fusion.14
  17.2 5.5 fusion.72
  28.0 2.8 fusion.6
  30.8 4.3 exponential_reduce_fusion.1
  35.1 2.6 convolution_convert_fusion
  38.3 6.8 fusion.7
  45.1 7.3 exponential_reduce_fusion
  52.5 4.1 fusion.24
  56.7 7.4 fusion.25
  66.0 5.8 fusion.81
  71.8 299.9 %all-gather.3.cloned.1.call-done = f32[4096,2048]{1,0:T(8,128)} async-done(((f32[1024,2048]{1,0:T(8,128)}), f32[4096,2048]{1,0:T(8,128)}) %all-gather.3.cloned.1.call-update) | async-done | bytes 33554448 | tf_op jit(solution)/shard_map/all_gather | solution.py:139
  371.7 16.1 reduce_sum.102
  387.9 5.7 multiply_reduce_fusion.2
  394.4 16.5 fusion.82
  410.9 13.4 fusion.83
  424.3 22.1 %multiply_convert_fusion.2 = (bf16[1024,2048]{1,0:T(8,128)(2,1)}, bf16[1024,2048]{1,0:T(8,128)(2,1)}, bf16[1024,2048]{1,0:T(8,128)(2,1)}) fusion(f32[1024,2048]{1,0:T(8,128)} %fusion.82, f32[1024,2048]{1,0:T(8,128)} %fusion.83, bf16[2048,2048]{1,0:T(8,128)(2,1)} %param.34, bf16[1024,2048]{1,0:T(8,128)(2,1)} %param.35, ...), kind=kOutput, calls=%fused_computation.30 | convolution fusion | flops 8625586176 | bytes 41944064 | tf_op jit(solution)/shard_map/dot_general | solution.py:153
  446.3 12.7 fusion.85
  459.1 13.7 convolution_add_fusion
  472.8 14.9 fusion.84
  487.7 157.2 %all-reduce.14.cloned.1.call-done = f32[1024,2048]{1,0:T(8,128)} async-done(((f32[1024,2048]{1,0:T(8,128)}), f32[1024,2048]{1,0:T(8,128)}) %all-reduce.14.cloned.1.call-update) | async-done | bytes 8388624 | tf_op jit(solution)/shard_map/psum | solution.py:163
  645.0 7.6 multiply_reduce_fusion
  652.6 9.5 multiply_add_fusion
  662.2 6.6 fusion.21
  669.3 4.0 convolution_bitcast_fusion
  673.4 7.5 multiply_convert_fusion.1
  680.9 5.6 convolution_bitcast_fusion.3
  688.2 7.4 fusion.19
  695.9 9.0 multiply_convert_fusion
  716.6 5.9 add_add_fusion
  723.2 7.2 fusion.64
  730.4 7.8 fusion.15
  738.3 7.0 fusion.66
  745.4 7.3 fusion.68
  752.9 15.6 fusion.88
  768.6 15.5 fusion.89
  784.4 15.6 fusion.62
  801.9 228.8 %all-reduce.16.cloned.1.call-done = (f32[1024,2048]{1,0:T(8,128)}, f32[1024,2048]{1,0:T(8,128)}) async-done(((f32[1024,2048]{1,0:T(8,128)}, f32[1024,2048]{1,0:T(8,128)}), (f32[1024,2048]{1,0:T(8,128)}, f32[1024,2048]{1,0:T(8,128)})) %all-reduce.16.cloned.1.call-update) | async-done | bytes 16777232 | tf_op jit(solution)/shard_map/psum | solution.py:149
  1030.7 5.9 fusion.13
  1036.5 29.6 %all-reduce.9 = (f32[2048]{0:T(1024)S(1)}, f32[2048]{0:T(1024)S(1)}) all-reduce(f32[2048]{0:T(1024)S(1)} %get-tuple-element.73, f32[2048]{0:T(1024)S(1)} %copy-done.47), channel_id=3, replica_groups=mesh['dp'=8,'tensor'=4] {'dp'}, use_global_device_ids=true, to_apply=%region_15.16.clone | all-reduce | flops 4096 | bytes 32768
  1067.4 9.6 add_convert_fusion
  1077.1 9.8 fusion.12
  1086.9 49.2 %reduce-scatter.14.cloned.1.call-done = f32[512,256]{1,0:T(8,128)} async-done(((f32[512,2048]{1,0:T(8,128)}), f32[512,256]{1,0:T(8,128)}) %reduce-scatter.14.cloned.1.call-update) | async-done | bytes 524304 | tf_op jit(solution)/shard_map/reduce_scatter | solution.py:239
  1136.1 51.1 %reduce-scatter.10.cloned.1.call-done = f32[256,512]{1,0:T(8,128)} async-done(((f32[2048,512]{1,0:T(8,128)}), f32[256,512]{1,0:T(8,128)}) %reduce-scatter.10.cloned.1.call-update) | async-done | bytes 524304 | tf_op jit(solution)/shard_map/reduce_scatter | solution.py:237
  1187.3 51.3 %reduce-scatter.8.cloned.1.call-done = f32[256,512]{1,0:T(8,128)} async-done(((f32[2048,512]{1,0:T(8,128)}), f32[256,512]{1,0:T(8,128)}) %reduce-scatter.8.cloned.1.call-update) | async-done | bytes 524304 | tf_op jit(solution)/shard_map/reduce_scatter | solution.py:236
  1238.5 169.6 %reduce-scatter.16.cloned.1.call-done = f32[256,2048]{1,0:T(8,128)} async-done(((f32[2048,2048]{1,0:T(8,128)}), f32[256,2048]{1,0:T(8,128)}) %reduce-scatter.16.cloned.1.call-update) | async-done | bytes 2097168 | tf_op jit(solution)/shard_map/reduce_scatter | solution.py:169
  1408.1 169.6 %reduce-scatter.18.cloned.1.call-done = f32[256,2048]{1,0:T(8,128)} async-done(((f32[2048,2048]{1,0:T(8,128)}), f32[256,2048]{1,0:T(8,128)}) %reduce-scatter.18.cloned.1.call-update) | async-done | bytes 2097168 | tf_op jit(solution)/shard_map/reduce_scatter | solution.py:170
  1577.7 169.4 %reduce-scatter.20.cloned.1.call-done = f32[2048,256]{1,0:T(8,128)} async-done(((f32[2048,2048]{1,0:T(8,128)}), f32[2048,256]{1,0:T(8,128)}) %reduce-scatter.20.cloned.1.call-update) | async-done | bytes 2097168 | tf_op jit(solution)/shard_map/reduce_scatter | solution.py:171
  (189 shorter events, 28.6 us)
Async XLA Ops:
  7.2 58.8 %copy-start = (bf16[512,2048]{1,0:T(8,128)(2,1)S(1)}, bf16[512,2048]{1,0:T(8,128)(2,1)}, u32[]{:S(2)}) copy-start(bf16[512,2048]{1,0:T(8,128)(2,1)} %param.30) | copy-start | bytes 6291460
  7.2 364.6 %all-gather.3.cloned.1.call-start = ((), (), s32[]{:S(2)}) async-start(), calls=%async_computation.15 | async-start | bytes 41943040 | tf_op jit(solution)/shard_map/all_gather | solution.py:139
  17.2 17.9 %copy-start.44 = (f32[1024]{0:T(1024)}, f32[1024]{0:T(1024)S(1)}, u32[]{:S(2)}) copy-start(f32[1024]{0:T(1024)S(1)} %add_rsqrt_fusion.1) | copy-start | bytes 12292
  27.3 10.9 copy-start.9
  27.3 10.9 copy-start.11
  27.4 10.9 copy-start.13
  27.4 10.9 copy-start.15
  28.0 24.5 %copy-start.19 = (pred[512,896]{1,0:T(8,128)(4,1)}, pred[512,896]{1,0:T(8,128)(4,1)S(1)}, u32[]{:S(2)}) copy-start(pred[512,896]{1,0:T(8,128)(4,1)S(1)} %and_and_fusion.1) | copy-start | bytes 1376260
  30.8 21.7 %copy-start.5 = (f32[8,512,896]{2,1,0:T(8,128)}, f32[8,512,896]{2,1,0:T(8,128)S(1)}, u32[]{:S(2)}) copy-start(f32[8,512,896]{2,1,0:T(8,128)S(1)} %get-tuple-element.127) | copy-start | bytes 44040196
  35.1 17.4 copy-start.52
  37.8 14.8 copy-start.39
  38.3 18.4 %copy-start.27 = (pred[512,896]{1,0:T(8,128)(4,1)}, pred[512,896]{1,0:T(8,128)(4,1)S(1)}, u32[]{:S(2)}) copy-start(pred[512,896]{1,0:T(8,128)(4,1)S(1)} %and_and_fusion) | copy-start | bytes 1376260
  56.7 7.5 copy-start.23
  71.8 573.2 %all-reduce.14.cloned.1.call-start = ((), (), s32[]{:S(2)}) async-start(), calls=%async_computation.7 | async-start | bytes 16777216 | tf_op jit(solution)/shard_map/psum | solution.py:163
  387.9 5.8 copy-start.43
  393.6 17.3 copy-start.2
  394.4 16.5 copy-start.17
  446.3 12.7 copy-start.58
  472.8 557.9 %all-reduce.16.cloned.1.call-start = ((), (), s32[]{:S(2)}) async-start(), calls=%async_computation.16 | async-start | bytes 33554432 | tf_op jit(solution)/shard_map/psum | solution.py:149
  644.9 7.6 copy-start.18
  652.6 16.7 slice-start
  652.6 16.7 slice-start.1
  652.6 16.7 slice-start.2
  662.1 6.7 copy-start.24
  662.1 6.7 copy-start.26
  662.1 7.1 slice-start.3
  662.1 7.1 copy-start.20
  662.1 7.1 copy-start.53
  668.9 19.3 %copy-start.42 = (bf16[512,512]{0,1:T(8,128)(2,1)}, bf16[512,512]{0,1:T(8,128)(2,1)S(1)}, u32[]{:S(2)}) copy-start(bf16[512,512]{0,1:T(8,128)(2,1)S(1)} %get-tuple-element.98) | copy-start | bytes 1572868
  673.4 7.6 copy-start.8
  680.9 5.6 copy-start.10
  680.9 5.6 copy-start.12
  688.2 7.6 copy-start.38
  695.8 9.0 copy-start.14
  695.9 9.0 copy-start.16
  722.5 7.9 copy-start.32
  722.5 364.4 %reduce-scatter.12.cloned.1.call-start = ((), (), s32[]{:S(2)}) async-start(), calls=%async_computation.10 | async-start | bytes 4718592 | tf_op jit(solution)/shard_map/reduce_scatter | solution.py:238
  730.4 7.9 copy-start.36
  730.4 405.7 %reduce-scatter.14.cloned.1.call-start = ((), (), s32[]{:S(2)}) async-start(), calls=%async_computation.11 | async-start | bytes 4718592 | tf_op jit(solution)/shard_map/reduce_scatter | solution.py:239
  738.2 7.2 copy-start.34
  738.3 449.0 %reduce-scatter.10.cloned.1.call-start = ((), (), s32[]{:S(2)}) async-start(), calls=%async_computation.9 | async-start | bytes 4718592 | tf_op jit(solution)/shard_map/reduce_scatter | solution.py:237
  745.4 493.2 %reduce-scatter.8.cloned.1.call-start = ((), (), s32[]{:S(2)}) async-start(), calls=%async_computation.8 | async-start | bytes 4718592 | tf_op jit(solution)/shard_map/reduce_scatter | solution.py:236
  752.7 655.4 %reduce-scatter.16.cloned.1.call-start = ((), (), s32[]{:S(2)}) async-start(), calls=%async_computation.12 | async-start | bytes 18874368 | tf_op jit(solution)/shard_map/reduce_scatter | solution.py:169
  768.5 809.2 %reduce-scatter.18.cloned.1.call-start = ((), (), s32[]{:S(2)}) async-start(), calls=%async_computation.13 | async-start | bytes 18874368 | tf_op jit(solution)/shard_map/reduce_scatter | solution.py:170
  784.1 963.0 %reduce-scatter.20.cloned.1.call-start = ((), (), s32[]{:S(2)}) async-start(), calls=%async_computation.14 | async-start | bytes 18874368 | tf_op jit(solution)/shard_map/reduce_scatter | solution.py:171
  800.0 236.5 %copy-start.47 = (f32[2048]{0:T(1024)S(1)}, f32[2048]{0:T(1024)}, u32[]{:S(2)}) copy-start(f32[2048]{0:T(1024)} %get-tuple-element.71) | copy-start | bytes 24580
  1067.4 9.6 copy-start.4
  1067.4 679.7 %copy-start.1 = (bf16[512,2048]{1,0:T(8,128)(2,1)S(1)}, bf16[512,2048]{1,0:T(8,128)(2,1)}, u32[]{:S(2)}) copy-start(bf16[512,2048]{1,0:T(8,128)(2,1)} %param.30) | copy-start | bytes 6291460
  (25 other events, 68.3 us)
Sparse Core Ops, SparseCore 0:
  71.9 299.7 all-gather.2
  472.9 172.0 all-reduce.13
  722.6 308.0 all-reduce.15
  1033.4 51.4 reduce-scatter.11
  1087.6 48.4 reduce-scatter.13
  1138.8 48.3 reduce-scatter.9
  1190.1 48.3 reduce-scatter.7
  1241.5 166.6 reduce-scatter.15
  1411.1 166.6 reduce-scatter.17
  1580.5 166.6 reduce-scatter.19
